TPU v7x, 32 devices: a whole 2x2x4 slice. The times are simulated.
32 devices in a mesh: grp: 4 (over y, x), frag: 8 (over z, core).
Axes of the slice: x: 2, y: 2, z: 4, core: 2. Of those that a mesh axis runs over, the one named last changes fastest.
Arguments:
- density: bfloat16 [64, 9216], P('frag'), may hold values from -0.1 to 1, as said below
- fock_blocks: bfloat16 [64, 9216], P('frag'), may hold values from -8 to 8, as said below
- coupling: bfloat16 [128, 9216], P(('grp', 'frag')), may hold values from -1.796875 to 1.796875
- dimer_pairs: int32 [128, 2], P(('grp', 'frag')), may hold values from 0 to 63, as said below
- atom_counts: int32 [64], P('frag'), may hold values from 8 to 16
- nuclear_charge: float32 [1024], P('frag'), may hold values from 4 to 12
- coords: float32 [3, 1024], P(None, 'frag'), may hold values from -120 to 120
Outputs:
- density_correction: float32 [64, 9216], P('frag')
- dimer_energy: float32 [128], P(('grp', 'frag'))
- total_energy: float32 [], replicated
Inputs may be any that keep to these rules, and one draw needn't show every extreme that they name: `dimer_pairs`: dimer d has fragments I < J; I // 8 == (d // 4) % 8, and J // 8 lies between I // 8 and I // 8 + 3. `density`: each row is a symmetric matrix. `fock_blocks`: each row is a symmetric matrix.
All inputs are finite; a program needn't handle non-finite values. Where the computation divides by a largest or mean magnitude, that divisor is 1e-20 or more.
Results may differ from a plain program's by a relative error of at most 0.0018.
Values may be sent and summed in bfloat16 or wider, within the bound.
A program may use at most 64 MiB of HBM per device.

v0:
```python
import jax
import jax.numpy as jnp
from jax import lax
from jax.sharding import PartitionSpec as P

NB = 96
NA = 16
REACH = 3
PURIF = 12


FULL_PRECISION = lax.Precision.HIGHEST


def from_behind(value, axis, steps):
    count = lax.axis_size(axis)
    first, last = (max(0, -steps), min(count, count - steps))
    return lax.ppermute(value, axis, [(source, source + steps) for source in range(first, last)])


def shortened(value):

    def short(part):
        return part.astype(jnp.bfloat16) if part.dtype == jnp.float32 else part

    return jax.tree.map(short, value)


def basis_atoms(count_real):
    basis_index = jnp.arange(NB, dtype=jnp.float32)[None, :, None]
    atom_index = jnp.arange(NA, dtype=jnp.float32)[None, None, :]
    scaled = basis_index * count_real[:, None, None]
    inside = jnp.logical_and(atom_index * NB <= scaled, scaled < (atom_index + 1.0) * NB)
    return inside.astype(jnp.float32)


def atom_table(density, nuclear_charge, atom_counts, coords):
    frag_count = density.shape[0]
    count_real = atom_counts.astype(jnp.float32)
    owners = basis_atoms(count_real)
    blocks = density.reshape(frag_count, NB, NB).astype(jnp.float32)
    on_diagonal = jnp.diagonal(blocks, axis1=1, axis2=2)
    population = 2.0 * jnp.sum(on_diagonal[:, :, None] * owners, axis=1)
    is_live = (jnp.arange(NA, dtype=jnp.float32)[None, :] < count_real[:, None]).astype(jnp.float32)
    charge = is_live * nuclear_charge.reshape(frag_count, NA) - population
    return jnp.concatenate([charge.reshape(1, -1), coords, is_live.reshape(1, -1)], axis=0)


def embed_potential(receivers, pair_ids, atom_rows):
    source_frag = jnp.arange(atom_rows.shape[1], dtype=jnp.int32) // NA
    keep_mask = jnp.logical_and(source_frag != pair_ids[0], source_frag != pair_ids[1]).astype(
        jnp.float32
    )
    offsets = receivers[1:4, :, None] - atom_rows[1:4, None, :]
    distance_sq = jnp.sum(offsets * offsets, axis=0)
    return jnp.sum((keep_mask * atom_rows[0])[None, :] / jnp.sqrt(distance_sq + 1.0), axis=1)


def dimer_solve(dens_pair, fock_pair, coupling_row, potential, count_pair):
    owners = basis_atoms(count_pair)
    site_shift = jnp.sum(owners * potential.reshape(2, 1, NA), axis=2)
    dens_blocks = dens_pair.astype(jnp.float32).reshape(2, NB, NB)
    fock_parts = fock_pair.astype(jnp.float32).reshape(2, NB, NB)
    cross_block = coupling_row.astype(jnp.float32).reshape(NB, NB)
    small_eye = jnp.eye(NB, dtype=jnp.float32)
    top_rows = jnp.concatenate(
        [fock_parts[0] + small_eye * site_shift[0][None, :], cross_block], axis=1
    )
    low_rows = jnp.concatenate(
        [cross_block.T, fock_parts[1] + small_eye * site_shift[1][None, :]], axis=1
    )
    dimer_fock = jnp.concatenate([top_rows, low_rows], axis=0)
    identity = jnp.eye(2 * NB, dtype=jnp.float32)
    centre = jnp.trace(dimer_fock) / (2.0 * NB)
    shifted = dimer_fock - centre * identity
    width = jnp.max(jnp.sum(jnp.abs(shifted), axis=1)) + 1e-06
    start = 0.5 * identity - shifted / (2.0 * width)

    def purify(index, current):
        square = jnp.dot(current, current, precision=FULL_PRECISION)
        return 3.0 * square - 2.0 * jnp.dot(square, current, precision=FULL_PRECISION)

    purified = lax.fori_loop(0, PURIF, purify, start)
    zero_block = jnp.zeros((NB, NB), jnp.float32)
    start_guess = jnp.concatenate(
        [
            jnp.concatenate([dens_blocks[0], zero_block], axis=1),
            jnp.concatenate([zero_block, dens_blocks[1]], axis=1),
        ],
        axis=0,
    )
    energy = jnp.sum((purified - start_guess) * dimer_fock.T)
    changes = jnp.stack([purified[:NB, :NB] - dens_blocks[0], purified[NB:, NB:] - dens_blocks[1]])
    return (changes.reshape(2, NB * NB), energy)


def per_device(density, fock_blocks, coupling, dimer_pairs, atom_counts, nuclear_charge, coords):
    frag_dev = density.shape[0]
    local_rows = atom_table(density, nuclear_charge, atom_counts, coords)
    atom_rows = lax.all_gather(local_rows, "frag", axis=1, tiled=True)
    my_index = lax.axis_index("frag")
    dens_list = [density]
    fock_list = [fock_blocks]
    for distance in range(1, REACH + 1):
        got_dens, got_fock = from_behind((density, fock_blocks), "frag", -distance)
        dens_list.append(got_dens)
        fock_list.append(got_fock)
    held_dens = jnp.concatenate(dens_list, axis=0)
    held_fock = jnp.concatenate(fock_list, axis=0)
    first_row = my_index * frag_dev
    held_index = dimer_pairs - first_row

    def solve_one(pair_ids, row_pair, coupling_row):
        columns = (pair_ids[:, None] * NA + jnp.arange(NA, dtype=jnp.int32)[None, :]).reshape(-1)
        receivers = jnp.take(atom_rows, columns, axis=1)
        potential = embed_potential(receivers, pair_ids, atom_rows)
        count_pair = jnp.sum(receivers[4].reshape(2, NA), axis=1)
        return dimer_solve(
            jnp.take(held_dens, row_pair, axis=0),
            jnp.take(held_fock, row_pair, axis=0),
            coupling_row,
            potential,
            count_pair,
        )

    changes, energies = jax.vmap(solve_one)(dimer_pairs, held_index, coupling)
    held_count = held_dens.shape[0]
    selector = (
        jnp.arange(held_count, dtype=jnp.int32)[:, None] == held_index.reshape(1, -1)
    ).astype(jnp.float32)
    partial_value = jnp.dot(selector, changes.reshape(-1, NB * NB), precision=FULL_PRECISION)
    own_rows = partial_value[:frag_dev]
    for distance in range(1, REACH + 1):
        piece = partial_value[distance * frag_dev : (distance + 1) * frag_dev]
        own_rows = own_rows + from_behind(shortened(piece), "frag", distance).astype(piece.dtype)
    own_rows = lax.psum(own_rows, "grp")
    total_energy = lax.psum(jnp.sum(energies), ("grp", "frag"))
    return (own_rows, energies, total_energy)


def solution(mesh):
    return jax.shard_map(
        per_device,
        mesh=mesh,
        in_specs=(
            P("frag", None),
            P("frag", None),
            P(("grp", "frag"), None),
            P(("grp", "frag"), None),
            P("frag"),
            P("frag"),
            P(None, "frag"),
        ),
        out_specs=(P("frag", None), P(("grp", "frag")), P()),
        check_vma=False,
    )
```

profile of v0, /device:TPU:18, one launch (start us, length us, event | category | flops | bytes accessed | tf_op | source)
XLA Modules:
  0.0 147.2 jit_solution(11617961245593250608)
XLA Ops:
  7.2 1.9 %collective-permute-start = (bf16[8,9216]{1,0:T(8,128)(2,1)}, bf16[8,9216]{1,0:T(8,128)(2,1)S(1)}, u32[]{:S(2)}, u32[]{:S(2)}) collective-permute-start(bf16[8,9216]{1,0:T(8,128)(2,1)} %param.12), channel_id=1, source_target_pairs={{1,0},{2,1},{3,2},{4,3},{5,4},{6,5},{7,6},{9,8},{10,9},{11,10},{12... | collective-permute-start | bytes 442376 | tf_op jit(solution)/shard_map/ppermute | solution.py:18
  9.1 2.4 %collective-permute-start.1 = (bf16[8,9216]{1,0:T(8,128)(2,1)}, bf16[8,9216]{1,0:T(8,128)(2,1)S(1)}, u32[]{:S(2)}, u32[]{:S(2)}) collective-permute-start(bf16[8,9216]{1,0:T(8,128)(2,1)} %param.12), channel_id=1, source_target_pairs={{2,0},{3,1},{4,2},{5,3},{6,4},{7,5},{10,8},{11,9},{12,10},{13,11},... | collective-permute-start | bytes 442376 | tf_op jit(solution)/shard_map/ppermute | solution.py:18
  11.5 1.9 %collective-permute-start.2 = (bf16[8,9216]{1,0:T(8,128)(2,1)}, bf16[8,9216]{1,0:T(8,128)(2,1)S(1)}, u32[]{:S(2)}, u32[]{:S(2)}) collective-permute-start(bf16[8,9216]{1,0:T(8,128)(2,1)} %param.12), channel_id=1, source_target_pairs={{3,0},{4,1},{5,2},{6,3},{7,4},{11,8},{12,9},{13,10},{14,11},{15,12... | collective-permute-start | bytes 442376 | tf_op jit(solution)/shard_map/ppermute | solution.py:18
  13.4 2.2 %collective-permute-start.3 = (bf16[8,9216]{1,0:T(8,128)(2,1)}, bf16[8,9216]{1,0:T(8,128)(2,1)S(1)}, u32[]{:S(2)}, u32[]{:S(2)}) collective-permute-start(bf16[8,9216]{1,0:T(8,128)(2,1)} %param.11), channel_id=1, source_target_pairs={{1,0},{2,1},{3,2},{4,3},{5,4},{6,5},{7,6},{9,8},{10,9},{11,10},{12... | collective-permute-start | bytes 442376 | tf_op jit(solution)/shard_map/ppermute | solution.py:18
  15.6 1.9 %collective-permute-start.4 = (bf16[8,9216]{1,0:T(8,128)(2,1)}, bf16[8,9216]{1,0:T(8,128)(2,1)S(1)}, u32[]{:S(2)}, u32[]{:S(2)}) collective-permute-start(bf16[8,9216]{1,0:T(8,128)(2,1)} %param.11), channel_id=1, source_target_pairs={{2,0},{3,1},{4,2},{5,3},{6,4},{7,5},{10,8},{11,9},{12,10},{13,11},... | collective-permute-start | bytes 442376 | tf_op jit(solution)/shard_map/ppermute | solution.py:18
  17.6 3.4 %copy.94 = f32[8,9216]{0,1:T(8,128)} copy(bf16[8,9216]{1,0:T(8,128)(2,1)} %param.11) | data formatting | bytes 442368 | tf_op jit(solution)/shard_map/convert_element_type | solution.py:41
  21.5 2.9 %gather_fusion = f32[96,8]{1,0:T(8,128)S(1)} fusion(f32[8,96,96]{0,2,1:T(8,128)} %bitcast.61, s32[96]{0:T(128)S(1)} %or_bitcast_fusion), kind=kCustom, calls=%fused_computation.2 | custom fusion | bytes 6912 | tf_op jit(solution)/shard_map/jit(diagonal)/gather | solution.py:42
  25.1 13.4 %all_gather.3 = f32[5,1024]{0,1:T(8,128)S(1)} all-gather(f32[5,128]{0,1:T(8,128)S(1)} %copy.96), channel_id=1, replica_groups=mesh['grp'=4,'frag'=8] {'frag'}, dimensions={1}, use_global_device_ids=true | all-gather | bytes 23040 | tf_op jit(solution)/shard_map/all_gather | solution.py:100
  39.2 0.6 gather_fusion.1
  42.0 4.1 %collective-permute-start.5 = (bf16[8,9216]{1,0:T(8,128)(2,1)S(1)}, bf16[8,9216]{1,0:T(8,128)(2,1)S(1)}, u32[]{:S(2)}, u32[]{:S(2)}) collective-permute-start(bf16[8,9216]{1,0:T(8,128)(2,1)S(1)} %copy-done), channel_id=1, source_target_pairs={{3,0},{4,1},{5,2},{6,3},{7,4},{11,8},{12,9},{13,10},{14,11},{15,12... | collective-permute-start | bytes 442376 | tf_op jit(solution)/shard_map/ppermute | solution.py:18
  46.2 0.6 gather_fusion.2
  47.0 4.6 %collective-permute-done.5 = bf16[8,9216]{1,0:T(8,128)(2,1)S(1)} collective-permute-done((bf16[8,9216]{1,0:T(8,128)(2,1)S(1)}, bf16[8,9216]{1,0:T(8,128)(2,1)S(1)}, u32[]{:S(2)}, u32[]{:S(2)}) %collective-permute-start.5) | collective-permute-done | bytes 147488 | tf_op jit(solution)/shard_map/ppermute | solution.py:18
  54.3 23.0 %while.10 = (s32[]{:T(128)}, f32[4,192,192]{2,1,0:T(8,128)S(1)}, s32[]{:T(128)}) while((s32[]{:T(128)}, f32[4,192,192]{2,1,0:T(8,128)S(1)}, s32[]{:T(128)}) %tuple.37), condition=%wide.region_9.11_spmd, body=%wide.region_8.10_spmd.sunk | while | flops 679919616 | bytes 4128813 | solution.py:83
  54.4 0.9 fusion.41
  55.3 0.9 fusion.42
  56.3 0.9 fusion.41
  57.2 0.9 fusion.42
  58.3 0.9 fusion.41
  59.2 0.9 fusion.42
  60.2 0.9 fusion.41
  61.1 0.9 fusion.42
  62.1 0.9 fusion.41
  63.0 0.9 fusion.42
  64.0 0.9 fusion.41
  64.9 0.9 fusion.42
  65.9 0.9 fusion.41
  66.8 0.9 fusion.42
  67.8 0.9 fusion.41
  68.7 0.9 fusion.42
  69.8 0.9 fusion.41
  70.6 0.9 fusion.42
  71.7 0.9 fusion.41
  72.6 0.9 fusion.42
  73.6 0.9 fusion.41
  74.5 0.9 fusion.42
  75.5 0.9 fusion.41
  76.4 0.9 fusion.42
  79.4 1.9 %collective-permute-start.6 = (bf16[8,9216]{1,0:T(8,128)(2,1)S(1)}, bf16[8,9216]{1,0:T(8,128)(2,1)S(1)}, u32[]{:S(2)}, u32[]{:S(2)}) collective-permute-start(bf16[8,9216]{1,0:T(8,128)(2,1)S(1)} %get-tuple-element.29), channel_id=1, source_target_pairs={{0,1},{1,2},{2,3},{3,4},{4,5},{5,6},{6,7},{8,9},{9,10},{10,11},{11... | collective-permute-start | bytes 442376 | tf_op jit(solution)/shard_map/ppermute | solution.py:18
  81.4 1.9 %collective-permute-start.7 = (bf16[8,9216]{1,0:T(8,128)(2,1)S(1)}, bf16[8,9216]{1,0:T(8,128)(2,1)S(1)}, u32[]{:S(2)}, u32[]{:S(2)}) collective-permute-start(bf16[8,9216]{1,0:T(8,128)(2,1)S(1)} %get-tuple-element.31), channel_id=1, source_target_pairs={{0,2},{1,3},{2,4},{3,5},{4,6},{5,7},{8,10},{9,11},{10,12},{11,13},... | collective-permute-start | bytes 442376 | tf_op jit(solution)/shard_map/ppermute | solution.py:18
  83.3 1.9 %collective-permute-start.8 = (bf16[8,9216]{1,0:T(8,128)(2,1)S(1)}, bf16[8,9216]{1,0:T(8,128)(2,1)S(1)}, u32[]{:S(2)}, u32[]{:S(2)}) collective-permute-start(bf16[8,9216]{1,0:T(8,128)(2,1)S(1)} %get-tuple-element.30), channel_id=1, source_target_pairs={{0,3},{1,4},{2,5},{3,6},{4,7},{8,11},{9,12},{10,13},{11,14},{12,15... | collective-permute-start | bytes 442376 | tf_op jit(solution)/shard_map/ppermute | solution.py:18
  85.2 0.7 collective-permute-done.6
  85.9 4.5 %collective-permute-done.7 = bf16[8,9216]{1,0:T(8,128)(2,1)S(1)} collective-permute-done((bf16[8,9216]{1,0:T(8,128)(2,1)S(1)}, bf16[8,9216]{1,0:T(8,128)(2,1)S(1)}, u32[]{:S(2)}, u32[]{:S(2)}) %collective-permute-start.7) | collective-permute-done | bytes 147488 | tf_op jit(solution)/shard_map/ppermute | solution.py:18
  90.4 2.4 %collective-permute-done.8 = bf16[8,9216]{1,0:T(8,128)(2,1)S(1)} collective-permute-done((bf16[8,9216]{1,0:T(8,128)(2,1)S(1)}, bf16[8,9216]{1,0:T(8,128)(2,1)S(1)}, u32[]{:S(2)}, u32[]{:S(2)}) %collective-permute-start.8) | collective-permute-done | bytes 147488 | tf_op jit(solution)/shard_map/ppermute | solution.py:18
  92.8 0.8 fusion.4
  93.6 1.0 fusion.20
  94.6 41.7 %psum.15 = f32[]{:T(128)} all-reduce(f32[]{:T(128)} %get-tuple-element.19), channel_id=1, replica_groups=mesh['grp'=4,'frag'=8] {'grp','frag'}, use_global_device_ids=true, to_apply=%region_13.15 | all-reduce | flops 1 | bytes 8 | tf_op jit(solution)/shard_map/psum | solution.py:137
  136.3 2.4 %all-reduce.4.cloned.1.call-done = f32[8,9216]{1,0:T(8,128)} async-done(((f32[8,9216]{1,0:T(8,128)}), f32[8,9216]{1,0:T(8,128)}) %all-reduce.4.cloned.1.call-update) | async-done | bytes 294928 | tf_op jit(solution)/shard_map/psum | solution.py:136
  138.7 1.7 %copy.123 = f32[8,9216]{1,0:T(8,128)} copy(f32[8,9216]{1,0:T(8,128)} %all-reduce.4.cloned.1.call-done) | data formatting | bytes 589824
  (116 shorter events, 9.3 us)
Async XLA Ops:
  7.2 131.5 %all-reduce.4.cloned.1.call-start = ((), (), s32[]{:S(2)}) async-start(), calls=%async_computation | async-start | bytes 589824 | tf_op jit(solution)/shard_map/psum | solution.py:136
  7.2 34.8 %collective-permute-start = (bf16[8,9216]{1,0:T(8,128)(2,1)}, bf16[8,9216]{1,0:T(8,128)(2,1)S(1)}, u32[]{:S(2)}, u32[]{:S(2)}) collective-permute-start(bf16[8,9216]{1,0:T(8,128)(2,1)} %param.12), channel_id=1, source_target_pairs={{1,0},{2,1},{3,2},{4,3},{5,4},{6,5},{7,6},{9,8},{10,9},{11,10},{12... | collective-permute-start | bytes 442376 | tf_op jit(solution)/shard_map/ppermute | solution.py:18
  9.1 37.0 %collective-permute-start.1 = (bf16[8,9216]{1,0:T(8,128)(2,1)}, bf16[8,9216]{1,0:T(8,128)(2,1)S(1)}, u32[]{:S(2)}, u32[]{:S(2)}) collective-permute-start(bf16[8,9216]{1,0:T(8,128)(2,1)} %param.12), channel_id=1, source_target_pairs={{2,0},{3,1},{4,2},{5,3},{6,4},{7,5},{10,8},{11,9},{12,10},{13,11},... | collective-permute-start | bytes 442376 | tf_op jit(solution)/shard_map/ppermute | solution.py:18
  11.5 34.7 %collective-permute-start.2 = (bf16[8,9216]{1,0:T(8,128)(2,1)}, bf16[8,9216]{1,0:T(8,128)(2,1)S(1)}, u32[]{:S(2)}, u32[]{:S(2)}) collective-permute-start(bf16[8,9216]{1,0:T(8,128)(2,1)} %param.12), channel_id=1, source_target_pairs={{3,0},{4,1},{5,2},{6,3},{7,4},{11,8},{12,9},{13,10},{14,11},{15,12... | collective-permute-start | bytes 442376 | tf_op jit(solution)/shard_map/ppermute | solution.py:18
  13.4 33.5 %collective-permute-start.3 = (bf16[8,9216]{1,0:T(8,128)(2,1)}, bf16[8,9216]{1,0:T(8,128)(2,1)S(1)}, u32[]{:S(2)}, u32[]{:S(2)}) collective-permute-start(bf16[8,9216]{1,0:T(8,128)(2,1)} %param.11), channel_id=1, source_target_pairs={{1,0},{2,1},{3,2},{4,3},{5,4},{6,5},{7,6},{9,8},{10,9},{11,10},{12... | collective-permute-start | bytes 442376 | tf_op jit(solution)/shard_map/ppermute | solution.py:18
  15.6 31.3 %collective-permute-start.4 = (bf16[8,9216]{1,0:T(8,128)(2,1)}, bf16[8,9216]{1,0:T(8,128)(2,1)S(1)}, u32[]{:S(2)}, u32[]{:S(2)}) collective-permute-start(bf16[8,9216]{1,0:T(8,128)(2,1)} %param.11), channel_id=1, source_target_pairs={{2,0},{3,1},{4,2},{5,3},{6,4},{7,5},{10,8},{11,9},{12,10},{13,11},... | collective-permute-start | bytes 442376 | tf_op jit(solution)/shard_map/ppermute | solution.py:18
  17.6 3.5 %copy-start.6 = (s32[8]{0:T(128)S(1)}, s32[8]{0:T(128)}, u32[]{:S(2)}) copy-start(s32[8]{0:T(128)} %param.15) | copy-start | bytes 100
  17.6 3.6 %copy-start.3 = (s32[4,2]{0,1:T(2,128)S(1)}, s32[4,2]{0,1:T(2,128)}, u32[]{:S(2)}) copy-start(s32[4,2]{0,1:T(2,128)} %param.14) | copy-start | bytes 100
  17.6 7.4 %copy-start.5 = (f32[128]{0:T(128)S(1)}, f32[128]{0:T(128)}, u32[]{:S(2)}) copy-start(f32[128]{0:T(128)} %param.16) | copy-start | bytes 1540
  17.6 7.4 %copy-start.4 = (f32[3,128]{1,0:T(4,128)S(1)}, f32[3,128]{1,0:T(4,128)}, u32[]{:S(2)}) copy-start(f32[3,128]{1,0:T(4,128)} %param.17) | copy-start | bytes 4612
  39.0 2.7 %copy-start.2 = (bf16[4,9216]{1,0:T(4,128)(2,1)S(1)}, bf16[4,9216]{1,0:T(4,128)(2,1)}, u32[]{:S(2)}) copy-start(bf16[4,9216]{1,0:T(4,128)(2,1)} %param.13) | copy-start | bytes 221188
  40.1 1.9 %copy-start = (bf16[8,9216]{1,0:T(8,128)(2,1)S(1)}, bf16[8,9216]{1,0:T(8,128)(2,1)}, u32[]{:S(2)}) copy-start(bf16[8,9216]{1,0:T(8,128)(2,1)} %param.11) | copy-start | bytes 442372
  40.1 6.1 %copy-start.1 = (bf16[8,9216]{1,0:T(8,128)(2,1)S(1)}, bf16[8,9216]{1,0:T(8,128)(2,1)}, u32[]{:S(2)}) copy-start(bf16[8,9216]{1,0:T(8,128)(2,1)} %param.12) | copy-start | bytes 442372
  42.0 9.6 %collective-permute-start.5 = (bf16[8,9216]{1,0:T(8,128)(2,1)S(1)}, bf16[8,9216]{1,0:T(8,128)(2,1)S(1)}, u32[]{:S(2)}, u32[]{:S(2)}) collective-permute-start(bf16[8,9216]{1,0:T(8,128)(2,1)S(1)} %copy-done), channel_id=1, source_target_pairs={{3,0},{4,1},{5,2},{6,3},{7,4},{11,8},{12,9},{13,10},{14,11},{15,12... | collective-permute-start | bytes 442376 | tf_op jit(solution)/shard_map/ppermute | solution.py:18
  79.4 6.5 %collective-permute-start.6 = (bf16[8,9216]{1,0:T(8,128)(2,1)S(1)}, bf16[8,9216]{1,0:T(8,128)(2,1)S(1)}, u32[]{:S(2)}, u32[]{:S(2)}) collective-permute-start(bf16[8,9216]{1,0:T(8,128)(2,1)S(1)} %get-tuple-element.29), channel_id=1, source_target_pairs={{0,1},{1,2},{2,3},{3,4},{4,5},{5,6},{6,7},{8,9},{9,10},{10,11},{11... | collective-permute-start | bytes 442376 | tf_op jit(solution)/shard_map/ppermute | solution.py:18
  81.4 9.1 %collective-permute-start.7 = (bf16[8,9216]{1,0:T(8,128)(2,1)S(1)}, bf16[8,9216]{1,0:T(8,128)(2,1)S(1)}, u32[]{:S(2)}, u32[]{:S(2)}) collective-permute-start(bf16[8,9216]{1,0:T(8,128)(2,1)S(1)} %get-tuple-element.31), channel_id=1, source_target_pairs={{0,2},{1,3},{2,4},{3,5},{4,6},{5,7},{8,10},{9,11},{10,12},{11,13},... | collective-permute-start | bytes 442376 | tf_op jit(solution)/shard_map/ppermute | solution.py:18
  83.3 9.5 %collective-permute-start.8 = (bf16[8,9216]{1,0:T(8,128)(2,1)S(1)}, bf16[8,9216]{1,0:T(8,128)(2,1)S(1)}, u32[]{:S(2)}, u32[]{:S(2)}) collective-permute-start(bf16[8,9216]{1,0:T(8,128)(2,1)S(1)} %get-tuple-element.30), channel_id=1, source_target_pairs={{0,3},{1,4},{2,5},{3,6},{4,7},{8,11},{9,12},{10,13},{11,14},{12,15... | collective-permute-start | bytes 442376 | tf_op jit(solution)/shard_map/ppermute | solution.py:18
Sparse Core Ops, SparseCore 0:
  93.7 44.9 all-reduce.3
where the time goes:
time: 149 us; the launch traced here: 147 us
  blocking collectives  55.2 us (37%)
  matrix products  22.5 us (15%)
  starting transfers between devices  20.2 us (14%)
  local copies, waits for them, and re-layouts  14.8 us (10%)
  waiting for transfers between devices  14.6 us (10%)
  between operations  14.6 us (10%)
  other arithmetic  4.93 us (3%)
    psum x1, blocking collectives, per_device(): total_energy = lax.psum(jnp.sum(energies), ('grp', 'frag'))  41.7 us
    ppermute x9, starting transfers between devices, from_behind(): lax.ppermute(value, axis, [(source, source + steps) for source in range(f...  20.2 us
    all_gather x1, blocking collectives, per_device(): atom_rows = lax.all_gather(local_rows, 'frag', axis=1, tiled=True)  13.4 us
    ppermute x9, waiting for transfers between devices, from_behind(): lax.ppermute(value, axis, [(source, source + steps) for source in range(f...  12.2 us
    dot_general x12, matrix products, purify(): jnp.dot(square, current, precision=FULL_PRECISION)  11.2 us
    dot_general x12, matrix products, purify(): square = jnp.dot(current, current, precision=FULL_PRECISION)  10.7 us
    convert_element_type x1, local copies, waits for them, and re-layouts, atom_table(): blocks = density.reshape(frag_count, NB, NB).astype(jnp.float32)  3.4 us
    gather x2, local copies, waits for them, and re-layouts, atom_table(): on_diagonal = jnp.diagonal(blocks, axis1=1, axis2=2)  2.99 us
  transfers between devices with their start and end apart: 10, of which 5 were waited for; matrix products, arithmetic and copies ran while one was open for 8% of the time, Pallas kernels for 0%

commit v1 on v0

v1 whole, which is shorter than its diff:
```python
import functools

import jax
import jax.numpy as jnp
from jax import lax
from jax.experimental import pallas as pl
from jax.experimental.pallas import tpu as pltpu
from jax.sharding import PartitionSpec as P

NB = 96
NA = 16
REACH = 3
PURIF = 12
LANES = 128
F32 = jnp.float32
BF16 = jnp.bfloat16


def iota(shape, dim):
    return lax.broadcasted_iota(jnp.int32, shape, dim)


def split(value):
    high = value.astype(BF16)
    return high, (value - high.astype(F32)).astype(BF16)


def dot(left, right):
    return jnp.dot(left, right, preferred_element_type=F32)


def product3(left, right):
    lh, ll = left
    rh, rl = right
    return dot(lh, rh) + (dot(lh, rl) + dot(ll, rh))


def remote(src, dst, send, recv, axis, index):
    return pltpu.make_async_remote_copy(
        src_ref=src,
        dst_ref=dst,
        send_sem=send,
        recv_sem=recv,
        device_id={axis: index},
        device_id_type=pl.DeviceIdType.MESH,
    )


def kernel(
    nf, ng, pairs, fock, dens, coup, count, nuc, xyz,
    out, eng_out, tot_out,
    tbl, tbl_t, halo, ys, fds, jsend, jrecv, acc, rs_recv, fin, e_all, g_all,
    t_s, t_r, h_s, h_r, j_s, j_r, r_s, r_r, a_s, a_r, e_s, e_r, g_s, g_r,
):
    fd = fock.shape[0]
    nd = coup.shape[0]
    ck = fd // ng
    me = lax.axis_index("frag")
    mg = lax.axis_index("grp")

    barrier = pltpu.get_barrier_semaphore()
    for k in range(1, nf):
        pl.semaphore_signal(barrier, inc=1, device_id={"frag": lax.rem(me + k, nf)}, device_id_type=pl.DeviceIdType.MESH)
    for k in range(1, ng):
        pl.semaphore_signal(barrier, inc=1, device_id={"grp": lax.rem(mg + k, ng)}, device_id_type=pl.DeviceIdType.MESH)

    lane = iota((1, LANES), 1)
    slot = lane & (NA - 1)
    part = lane >> 4
    cnt = count[...]
    scaled = iota((NB, LANES), 0) * cnt
    owned = jnp.logical_and(slot * NB <= scaled, scaled < (slot + 1) * NB)
    eye = iota((NB, NB), 0) == iota((NB, NB), 1)
    gathered = jnp.zeros((NB, LANES), F32)
    own_energy = jnp.zeros((1, LANES), F32)
    for k in range(fd):
        dk = dens[k].astype(F32)
        fk = fock[k].astype(F32)
        diag = jnp.sum(jnp.where(eye, dk, 0.0), axis=1, keepdims=True)
        gathered += jnp.where(jnp.logical_and(owned, part == k), diag, 0.0)
        value = jnp.sum(jnp.sum(dk * fk, axis=0, keepdims=True), axis=1, keepdims=True)
        own_energy = jnp.where(part == k, value, own_energy)
    pop = jnp.sum(gathered, axis=0, keepdims=True)
    ids = jnp.zeros((1, LANES), F32)
    for t in range(nd):
        ids = jnp.where(lane == t, pairs[t, 1].astype(F32), ids)
        ids = jnp.where(lane == nd + t, pairs[t, 0].astype(F32), ids)
    tbl[me, 0:1, :] = jnp.where(slot < cnt, nuc[...], 0.0) - 2.0 * pop
    tbl[me, 1:4, :] = xyz[...]
    tbl[me, 4:5, :] = cnt.astype(F32)
    tbl[me, 5:6, :] = pop
    tbl[me, 6:7, :] = own_energy
    tbl[me, 7:8, :] = ids
    for k in range(fd):
        halo[k] = fock[k]

    pl.semaphore_wait(barrier, nf + ng - 2)

    tcopies = []
    for k in range(1, nf):
        copy = remote(tbl.at[me], tbl.at[me], t_s.at[k], t_r.at[k], "frag", lax.rem(me + k, nf))
        copy.start()
        tcopies.append(copy)
    hcopies = []
    for d in range(1, REACH + 1):
        copy = remote(fock, halo.at[pl.ds(d * fd, fd)], h_s.at[d], h_r.at[d], "frag", lax.rem(me + nf - d, nf))
        hcopies.append(copy)
        pl.when(me >= d)(copy.start)

    for copy in tcopies:
        copy.wait_recv()
    for c in range(nf):
        tbl_t[pl.ds(c * fd, fd)] = jnp.transpose(tbl[c]).reshape(fd, NA, 8)

    source_part = part
    shifts = []
    off_energy = []
    for t in range(nd):
        first, second = pairs[t, 0], pairs[t, 1]
        rows = jnp.concatenate([tbl_t[first], tbl_t[second]], axis=0)
        total = jnp.zeros((2 * NA, LANES), F32)
        for c in range(nf):
            tile = tbl[c]
            ids_here = source_part + c * fd
            keep = jnp.logical_and(ids_here != first, ids_here != second)
            charge = jnp.where(keep, tile[0:1, :], 0.0)
            dx = rows[:, 1:2] - tile[1:2, :]
            dy = rows[:, 2:3] - tile[2:3, :]
            dz = rows[:, 3:4] - tile[3:4, :]
            total += charge * lax.rsqrt(dx * dx + dy * dy + dz * dz + 1.0)
        pot = jnp.sum(total, axis=1, keepdims=True)
        pair_shift = []
        atom = iota((NA, NB), 0)
        basis = iota((NA, NB), 1).astype(F32)
        for h in range(2):
            n_here = rows[h * NA : h * NA + 1, 4:5]
            s = basis * n_here
            low = (atom * NB).astype(F32)
            inside = jnp.logical_and(low <= s, s < low + float(NB))
            pair_shift.append(jnp.sum(jnp.where(inside, pot[h * NA : (h + 1) * NA], 0.0), axis=0, keepdims=True))
        shifts.append(pair_shift)
        off = jnp.sum(pot * rows[:, 5:6], axis=0, keepdims=True)
        off_energy.append(off + rows[0:1, 6:7] + rows[NA : NA + 1, 6:7])

    for d in range(1, REACH + 1):
        pl.when(me + d < nf)(hcopies[d - 1].wait_recv)

    big_eye = iota((2 * NB, 2 * NB), 0) == iota((2 * NB, 2 * NB), 1)
    for t in range(nd):
        first, second = pairs[t, 0], pairs[t, 1]
        fi = halo[jnp.clip(first - me * fd, 0, fd - 1)].astype(F32) + jnp.where(eye, shifts[t][0], 0.0)
        fj = halo[jnp.clip(second - me * fd, 0, (REACH + 1) * fd - 1)].astype(F32) + jnp.where(eye, shifts[t][1], 0.0)
        cross = coup[t].astype(F32)
        full = jnp.concatenate(
            [jnp.concatenate([fi, cross], axis=1), jnp.concatenate([jnp.transpose(cross), fj], axis=1)], axis=0
        )
        fds[t] = full
        trace = jnp.sum(jnp.sum(jnp.where(big_eye, full, 0.0), axis=0, keepdims=True), axis=1, keepdims=True)
        shifted = full - jnp.where(big_eye, trace / (2.0 * NB), 0.0)
        width = jnp.max(jnp.sum(jnp.abs(shifted), axis=0, keepdims=True), axis=1, keepdims=True) + 1e-06
        ys[t] = -shifted / width

    def purify(index, carry):
        for t in range(nd):
            y = ys[t]
            halves = split(y)
            square = product3(halves, halves)
            ys[t] = 1.5 * y - 0.5 * product3(split(square), halves)
        return carry

    lax.fori_loop(0, PURIF, purify, 0)

    energies = jnp.zeros((1, LANES), F32)
    iblocks = []
    jblocks = []
    for t in range(nd):
        y = ys[t]
        full = fds[t]
        trace = jnp.where(big_eye, full, 0.0)
        both = jnp.sum(jnp.sum(trace + y * full, axis=0, keepdims=True), axis=1, keepdims=True)
        energies = jnp.where(lane == t, 0.5 * both - off_energy[t], energies)
        iblocks.append(0.5 * y[:NB, :NB])
        jblock = 0.5 * y[NB:, NB:]
        jblocks.append(jblock)
        jsend[t] = jblock.astype(BF16)
    e_all[me] = jnp.broadcast_to(energies, (8, LANES))
    eng_out[...] = energies

    for k in range(fd):
        base = jnp.where(eye, 0.5, 0.0) - dens[k].astype(F32)
        total = jnp.zeros((NB, NB), F32)
        for t in range(nd):
            here = (me * fd + k).astype(F32)
            total += jnp.where(ids[:, nd + t : nd + t + 1] == here, iblocks[t] + base, 0.0)
            total += jnp.where(ids[:, t : t + 1] == here, jblocks[t] + base, 0.0)
        acc[k] = total

    ecopies = []
    for k in range(1, nf):
        copy = remote(e_all.at[me], e_all.at[me], e_s.at[k], e_r.at[k], "frag", lax.rem(me + k, nf))
        copy.start()
        ecopies.append(copy)
    jcopies = []
    for d in range(1, REACH + 1):
        copy = remote(jsend, jrecv.at[d - 1], j_s.at[d], j_r.at[d], "frag", lax.rem(me + d, nf))
        jcopies.append(copy)
        pl.when(me + d < nf)(copy.start)

    for copy in ecopies:
        copy.wait_recv()
    group_sum = e_all[0]
    for c in range(1, nf):
        group_sum += e_all[c]
    g_all[mg] = group_sum
    for d in range(1, REACH + 1):

        @pl.when(me >= d)
        def _():
            jcopies[d - 1].wait_recv()
            sender = tbl[lax.rem(me + nf - d, nf)]
            for k in range(fd):
                base = jnp.where(eye, 0.5, 0.0) - dens[k].astype(F32)
                total = acc[k]
                for t in range(nd):
                    hit = sender[7:8, t : t + 1] == (me * fd + k).astype(F32)
                    total += jnp.where(hit, jrecv[d - 1, t].astype(F32) + base, 0.0)
                acc[k] = total

    rcopies = []
    for k in range(1, ng):
        peer = lax.rem(mg + k, ng)
        copy = remote(acc.at[pl.ds(peer * ck, ck)], rs_recv.at[k], r_s.at[k], r_r.at[k], "grp", peer)
        copy.start()
        rcopies.append(copy)
        copy = remote(g_all.at[mg], g_all.at[mg], g_s.at[k], g_r.at[k], "grp", peer)
        copy.start()
        rcopies.append(copy)
    for copy in rcopies:
        copy.wait_recv()
    mine = pl.ds(mg * ck, ck)
    total = acc[mine]
    for k in range(1, ng):
        total += rs_recv[k]
    fin[mine] = total
    whole = g_all[0]
    for c in range(1, ng):
        whole += g_all[c]
    tot_out[...] = jnp.sum(whole[0:1, :], axis=1, keepdims=True)
    acopies = []
    for k in range(1, ng):
        copy = remote(fin.at[mine], fin.at[mine], a_s.at[k], a_r.at[k], "grp", lax.rem(mg + k, ng))
        copy.start()
        acopies.append(copy)
    for copy in acopies:
        copy.wait_recv()
    out[...] = fin[...]

    for copy in tcopies + ecopies + rcopies + acopies:
        copy.wait_send()
    for d in range(1, REACH + 1):
        pl.when(me >= d)(hcopies[d - 1].wait_send)
        pl.when(me + d < nf)(jcopies[d - 1].wait_send)


def per_device(nf, ng, density, fock_blocks, coupling, dimer_pairs, atom_counts, nuclear_charge, coords):
    fd = density.shape[0]
    nd = coupling.shape[0]
    ck = fd // ng
    vmem = pl.BlockSpec(memory_space=pltpu.VMEM)
    smem = pl.BlockSpec(memory_space=pltpu.SMEM)
    sem = pltpu.SemaphoreType.DMA
    out, energies, total = pl.pallas_call(
        functools.partial(kernel, nf, ng),
        out_shape=(
            jax.ShapeDtypeStruct((fd, NB, NB), F32),
            jax.ShapeDtypeStruct((1, LANES), F32),
            jax.ShapeDtypeStruct((1, 1), F32),
        ),
        in_specs=[smem] + [vmem] * 6,
        out_specs=(vmem, vmem, vmem),
        scratch_shapes=[
            pltpu.VMEM((nf, 8, LANES), F32),
            pltpu.VMEM((nf * fd, NA, 8), F32),
            pltpu.VMEM(((REACH + 1) * fd, NB, NB), BF16),
            pltpu.VMEM((nd, 2 * NB, 2 * NB), F32),
            pltpu.VMEM((nd, 2 * NB, 2 * NB), F32),
            pltpu.VMEM((nd, NB, NB), BF16),
            pltpu.VMEM((REACH, nd, NB, NB), BF16),
            pltpu.VMEM((fd, NB, NB), F32),
            pltpu.VMEM((ng, ck, NB, NB), F32),
            pltpu.VMEM((fd, NB, NB), F32),
            pltpu.VMEM((nf, 8, LANES), F32),
            pltpu.VMEM((ng, 8, LANES), F32),
        ]
        + [sem((nf,))] * 2
        + [sem((REACH + 1,))] * 4
        + [sem((ng,))] * 4
        + [sem((nf,))] * 2
        + [sem((ng,))] * 2,
        compiler_params=pltpu.CompilerParams(collective_id=0, has_side_effects=True, vmem_limit_bytes=40 << 20),
        name="dimer_step",
    )(
        dimer_pairs,
        fock_blocks.reshape(fd, NB, NB),
        density.reshape(fd, NB, NB),
        coupling.reshape(nd, NB, NB),
        jnp.repeat(atom_counts, NA).reshape(1, LANES),
        nuclear_charge.reshape(1, LANES),
        coords,
    )
    return out.reshape(fd, NB * NB), energies[0, :nd], total[0, 0]


def solution(mesh):
    nf, ng = mesh.shape["frag"], mesh.shape["grp"]
    return jax.shard_map(
        functools.partial(per_device, nf, ng),
        mesh=mesh,
        in_specs=(
            P("frag", None),
            P("frag", None),
            P(("grp", "frag"), None),
            P(("grp", "frag"), None),
            P("frag"),
            P("frag"),
            P(None, "frag"),
        ),
        out_specs=(P("frag", None), P(("grp", "frag")), P()),
        check_vma=False,
    )
```

time: 149 us -> 62.2 us (0.42); the launches traced: 147 us -> 62 us
  blocking collectives: 55.2 us -> 0 us
  Pallas kernels: 0 us -> 54 us
  matrix products: 22.5 us -> 0 us
  starting transfers between devices: 20.2 us -> 0 us
  waiting for transfers between devices: 14.6 us -> 0 us
  between operations: 14.6 us -> 2.39 us
  local copies, waits for them, and re-layouts: 14.8 us -> 5.59 us
  other arithmetic: 4.93 us -> 0 us
    pallas_call x0 -> x1, Pallas kernels: none -> 54 us  [per_device(): pl.pallas_call(functools.partial(kernel, nf, ng), out_shape=(jax.ShapeDty...]
    psum x1 -> x0, blocking collectives: 41.7 us -> none  [per_device(): total_energy = lax.psum(jnp.sum(energies), ('grp', 'frag'))]
    dot_general x25 -> x0, matrix products: 22.5 us -> none  [the longest x12 11.2 us: purify(): jnp.dot(square, current, precision=FULL_PRECISION)]
    ppermute x9 -> x0, starting transfers between devices: 20.2 us -> none  [from_behind(): lax.ppermute(value, axis, [(source, source + steps) for source in range(f...]
    all_gather x1 -> x0, blocking collectives: 13.4 us -> none  [per_device(): atom_rows = lax.all_gather(local_rows, 'frag', axis=1, tiled=True)]
    ppermute x9 -> x0, waiting for transfers between devices: 12.2 us -> none  [from_behind(): lax.ppermute(value, axis, [(source, source + steps) for source in range(f...]
    gather x8 -> x0, local copies, waits for them, and re-layouts: 5.12 us -> none  [the longest x2 2.99 us: atom_table(): on_diagonal = jnp.diagonal(blocks, axis1=1, axis2=2)]
    convert_element_type x2 -> x0, local copies, waits for them, and re-layouts: 3.48 us -> none  [the longest x1 3.4 us: atom_table(): blocks = density.reshape(frag_count, NB, NB).astype(jnp.float32)]
  transfers between devices with their start and end apart: 10 -> 0, of which waited for: 5 -> 0; matrix products, arithmetic and copies ran while one was open for 8% -> 0% of each run, Pallas kernels for 0% -> 0%
where the time goes in v1:
time: 62.2 us; the launch traced here: 62 us
  Pallas kernels  54 us (87%)
  local copies, waits for them, and re-layouts  5.59 us (9%)
  between operations  2.39 us (4%)
    pallas_call x1, Pallas kernels, per_device(): pl.pallas_call(functools.partial(kernel, nf, ng), out_shape=(jax.ShapeDty...  54 us
    unnamed x11, local copies, waits for them, and re-layouts  1.96 us

profile of v1, /device:TPU:18, one launch (start us, length us, event | category | flops | bytes accessed | tf_op | source)
XLA Modules:
  0.0 62.0 jit_solution(10237158366003873650)
XLA Ops:
  0.6 0.0 copy-start.4
  0.6 0.0 copy-start.2
  0.6 0.7 %copy-done.4 = s32[4,2]{0,1:T(2,128)S(1)} copy-done((s32[4,2]{0,1:T(2,128)S(1)}, s32[4,2]{0,1:T(2,128)}, u32[]{:S(2)}) %copy-start.4) | copy-done | bytes 56
  1.3 0.1 copy.10.pairs
  1.4 0.7 %broadcast_in_dim.3 = s32[8,16]{1,0:T(8,128)S(1)} broadcast(s32[8]{0:T(128)} %param.11), dimensions={0} | broadcast | bytes 544 | tf_op jit(solution)/shard_map/broadcast_in_dim | solution.py:307
  2.1 0.1 reshape_reshape.3.count
  2.2 1.0 %reshape.23.coup = bf16[4,96,96]{2,1,0:T(8,128)(2,1)S(1)} reshape(bf16[4,9216]{1,0:T(4,128)(2,1)} %param.9) | data formatting | bytes 147456 | tf_op jit(solution)/shard_map/reshape | solution.py:306
  3.2 0.0 copy-done.2
  3.2 0.0 copy-start.3
  3.2 0.2 reshape.22.dens
  3.4 0.7 %copy-done.3 = bf16[8,9216]{1,0:T(8,128)(2,1)S(1)} copy-done((bf16[8,9216]{1,0:T(8,128)(2,1)S(1)}, bf16[8,9216]{1,0:T(8,128)(2,1)}, u32[]{:S(2)}) %copy-start.3) | copy-done | bytes 147480
  4.1 0.0 copy-start
  4.2 0.0 copy-start.1
  4.2 0.2 reshape.21.fock
  4.3 0.5 copy-done
  4.8 0.0 copy-done.1
  4.8 54.0 %dimer_step.1 = (f32[8,96,96]{2,1,0:T(8,128)S(1)}, f32[1,128]{1,0:T(1,128)S(1)}, f32[1,1]{1,0:T(1,128)}) custom-call(s32[4,2]{1,0:T(4,128)S(1)} %copy.10.pairs, bf16[8,96,96]{2,1,0:T(8,128)(2,1)S(1)} %reshape.21.fock, bf16[8,96,96]{2,1,0:T(8,128)(2,1)S(1)} %reshape.22.dens, bf16[4,96,96]{2,1,0:T(8,128)(2,1)S(1)} %reshape.23.coup, ...), custom_call_target="tpu_custom_call" | custom-call | tf_op jit(solution)/shard_map/dimer_step/pallas_call | solution.py:272
  58.8 0.9 %reshape.25 = f32[8,9216]{1,0:T(8,128)} reshape(f32[8,96,96]{2,1,0:T(8,128)S(1)} %get-tuple-element.6) | data formatting | bytes 589824 | tf_op jit(solution)/shard_map/reshape | solution.py:311
  59.8 0.5 slice_bitcast_fusion
Async XLA Ops:
  0.6 0.7 %copy-start.4 = (s32[4,2]{0,1:T(2,128)S(1)}, s32[4,2]{0,1:T(2,128)}, u32[]{:S(2)}) copy-start(s32[4,2]{0,1:T(2,128)} %param.10) | copy-start | bytes 100
  0.6 2.6 %copy-start.2 = (bf16[8,9216]{1,0:T(8,128)(2,1)S(1)}, bf16[8,9216]{1,0:T(8,128)(2,1)}, u32[]{:S(2)}) copy-start(bf16[8,9216]{1,0:T(8,128)(2,1)} %param.7) | copy-start | bytes 442372
  3.2 0.9 %copy-start.3 = (bf16[8,9216]{1,0:T(8,128)(2,1)S(1)}, bf16[8,9216]{1,0:T(8,128)(2,1)}, u32[]{:S(2)}) copy-start(bf16[8,9216]{1,0:T(8,128)(2,1)} %param.8) | copy-start | bytes 442372
  4.1 0.7 %copy-start = (f32[3,128]{1,0:T(4,128)S(1)}, f32[3,128]{1,0:T(4,128)}, u32[]{:S(2)}) copy-start(f32[3,128]{1,0:T(4,128)} %xyz.1) | copy-start | bytes 4612
  4.2 0.7 %copy-start.1 = (f32[128]{0:T(128)S(1)}, f32[128]{0:T(128)}, u32[]{:S(2)}) copy-start(f32[128]{0:T(128)} %param.12) | copy-start | bytes 1540

commit v2 on v1

--- a/solution.py
+++ b/solution.py
@@ -11,6 +11,7 @@
 NA = 16
 REACH = 3
 PURIF = 12
+EARLY = 6
 LANES = 128
 F32 = jnp.float32
 BF16 = jnp.bfloat16
@@ -33,6 +34,30 @@
     lh, ll = left
     rh, rl = right
     return dot(lh, rh) + (dot(lh, rl) + dot(ll, rh))
+
+
+def product1(left, right):
+    return dot(left.astype(BF16), right.astype(BF16))
+
+
+def grid():
+    return iota((NB, NB), 0), iota((NB, NB), 1)
+
+
+def pack(first, second):
+    row, col = grid()
+    diag = jnp.sum(jnp.where(row == col, second, 0.0), axis=1, keepdims=True)
+    return jnp.where(row <= col, first, second), jnp.broadcast_to(diag, (NB, LANES - NB))
+
+
+def unpack_first(main, flipped):
+    row, col = grid()
+    return jnp.where(row <= col, main, flipped)
+
+
+def unpack_second(main, flipped, diag):
+    row, col = grid()
+    return jnp.where(row > col, main, jnp.where(row == col, diag, flipped))
 
 
 def remote(src, dst, send, recv, axis, index):
@@ -49,12 +74,15 @@
 def kernel(
     nf, ng, pairs, fock, dens, coup, count, nuc, xyz,
     out, eng_out, tot_out,
-    tbl, tbl_t, halo, ys, fds, jsend, jrecv, acc, rs_recv, fin, e_all, g_all,
+    tbl, tbl_t, halo, ys, fds, jsend, jrecv, acc, rs_src, rs_recv, fin, e_all, g_all,
     t_s, t_r, h_s, h_r, j_s, j_r, r_s, r_r, a_s, a_r, e_s, e_r, g_s, g_r,
 ):
     fd = fock.shape[0]
+    fh = fd // 2
     nd = coup.shape[0]
     ck = fd // ng
+    paired = ck % 2 == 0
+    cu = ck // 2 if paired else ck
     me = lax.axis_index("frag")
     mg = lax.axis_index("grp")
 
@@ -67,7 +95,9 @@
     lane = iota((1, LANES), 1)
     slot = lane & (NA - 1)
     part = lane >> 4
-    cnt = count[...]
+    cnt = jnp.zeros((1, LANES), jnp.int32)
+    for k in range(fd):
+        cnt = jnp.where(part == k, count[k], cnt)
     scaled = iota((NB, LANES), 0) * cnt
     owned = jnp.logical_and(slot * NB <= scaled, scaled < (slot + 1) * NB)
     eye = iota((NB, NB), 0) == iota((NB, NB), 1)
@@ -83,16 +113,18 @@
     pop = jnp.sum(gathered, axis=0, keepdims=True)
     ids = jnp.zeros((1, LANES), F32)
     for t in range(nd):
-        ids = jnp.where(lane == t, pairs[t, 1].astype(F32), ids)
-        ids = jnp.where(lane == nd + t, pairs[t, 0].astype(F32), ids)
+        ids = jnp.where(lane == t, pairs[1, t].astype(F32), ids)
+        ids = jnp.where(lane == nd + t, pairs[0, t].astype(F32), ids)
     tbl[me, 0:1, :] = jnp.where(slot < cnt, nuc[...], 0.0) - 2.0 * pop
     tbl[me, 1:4, :] = xyz[...]
     tbl[me, 4:5, :] = cnt.astype(F32)
     tbl[me, 5:6, :] = pop
     tbl[me, 6:7, :] = own_energy
     tbl[me, 7:8, :] = ids
-    for k in range(fd):
-        halo[k] = fock[k]
+    for p in range(fh):
+        main, diag = pack(fock[2 * p].astype(F32), fock[2 * p + 1].astype(F32))
+        halo[p, :, 0:NB] = main.astype(BF16)
+        halo[p, :, NB:LANES] = diag.astype(BF16)
 
     pl.semaphore_wait(barrier, nf + ng - 2)
 
@@ -103,7 +135,7 @@
         tcopies.append(copy)
     hcopies = []
     for d in range(1, REACH + 1):
-        copy = remote(fock, halo.at[pl.ds(d * fd, fd)], h_s.at[d], h_r.at[d], "frag", lax.rem(me + nf - d, nf))
+        copy = remote(halo.at[pl.ds(0, fh)], halo.at[pl.ds(d * fh, fh)], h_s.at[d], h_r.at[d], "frag", lax.rem(me + nf - d, nf))
         hcopies.append(copy)
         pl.when(me >= d)(copy.start)
 
@@ -116,7 +148,7 @@
     shifts = []
     off_energy = []
     for t in range(nd):
-        first, second = pairs[t, 0], pairs[t, 1]
+        first, second = pairs[0, t], pairs[1, t]
         rows = jnp.concatenate([tbl_t[first], tbl_t[second]], axis=0)
         total = jnp.zeros((2 * NA, LANES), F32)
         for c in range(nf):
@@ -147,9 +179,15 @@
 
     big_eye = iota((2 * NB, 2 * NB), 0) == iota((2 * NB, 2 * NB), 1)
     for t in range(nd):
-        first, second = pairs[t, 0], pairs[t, 1]
-        fi = halo[jnp.clip(first - me * fd, 0, fd - 1)].astype(F32) + jnp.where(eye, shifts[t][0], 0.0)
-        fj = halo[jnp.clip(second - me * fd, 0, (REACH + 1) * fd - 1)].astype(F32) + jnp.where(eye, shifts[t][1], 0.0)
+        first, second = pairs[0, t], pairs[1, t]
+        fi = fock[jnp.clip(first - me * fd, 0, fd - 1)].astype(F32) + jnp.where(eye, shifts[t][0], 0.0)
+        where_j = jnp.clip(second - me * fd, 0, (REACH + 1) * fd - 1)
+        tile = halo[where_j >> 1].astype(F32)
+        main = tile[:, 0:NB]
+        flipped = jnp.transpose(main)
+        even = ((iota((NB, NB), 0) * 0 + where_j) & 1) == 0
+        fj = jnp.where(even, unpack_first(main, flipped), unpack_second(main, flipped, tile[:, NB : NB + 1]))
+        fj = fj + jnp.where(eye, shifts[t][1], 0.0)
         cross = coup[t].astype(F32)
         full = jnp.concatenate(
             [jnp.concatenate([fi, cross], axis=1), jnp.concatenate([jnp.transpose(cross), fj], axis=1)], axis=0
@@ -168,31 +206,40 @@
             ys[t] = 1.5 * y - 0.5 * product3(split(square), halves)
         return carry
 
-    lax.fori_loop(0, PURIF, purify, 0)
+    def purify_early(index, carry):
+        for t in range(nd):
+            y = ys[t]
+            ys[t] = 1.5 * y - 0.5 * product1(product1(y, y), y)
+        return carry
+
+    lax.fori_loop(0, EARLY, purify_early, 0)
+    lax.fori_loop(EARLY, PURIF, purify, 0)
 
     energies = jnp.zeros((1, LANES), F32)
-    iblocks = []
-    jblocks = []
+    for t in range(nd):
+        jsend[t] = (0.5 * ys[t, NB:, NB:]).astype(BF16)
     for t in range(nd):
         y = ys[t]
         full = fds[t]
         trace = jnp.where(big_eye, full, 0.0)
         both = jnp.sum(jnp.sum(trace + y * full, axis=0, keepdims=True), axis=1, keepdims=True)
         energies = jnp.where(lane == t, 0.5 * both - off_energy[t], energies)
-        iblocks.append(0.5 * y[:NB, :NB])
-        jblock = 0.5 * y[NB:, NB:]
-        jblocks.append(jblock)
-        jsend[t] = jblock.astype(BF16)
     e_all[me] = jnp.broadcast_to(energies, (8, LANES))
     eng_out[...] = energies
 
+    jcopies = []
+    for d in range(1, REACH + 1):
+        copy = remote(jsend, jrecv.at[d - 1], j_s.at[d], j_r.at[d], "frag", lax.rem(me + d, nf))
+        jcopies.append(copy)
+        pl.when(me + d < nf)(copy.start)
+
     for k in range(fd):
         base = jnp.where(eye, 0.5, 0.0) - dens[k].astype(F32)
+        here = (me * fd + k).astype(F32)
         total = jnp.zeros((NB, NB), F32)
         for t in range(nd):
-            here = (me * fd + k).astype(F32)
-            total += jnp.where(ids[:, nd + t : nd + t + 1] == here, iblocks[t] + base, 0.0)
-            total += jnp.where(ids[:, t : t + 1] == here, jblocks[t] + base, 0.0)
+            total += jnp.where(ids[:, nd + t : nd + t + 1] == here, 0.5 * ys[t, :NB, :NB] + base, 0.0)
+            total += jnp.where(ids[:, t : t + 1] == here, 0.5 * ys[t, NB:, NB:] + base, 0.0)
         acc[k] = total
 
     ecopies = []
@@ -200,11 +247,6 @@
         copy = remote(e_all.at[me], e_all.at[me], e_s.at[k], e_r.at[k], "frag", lax.rem(me + k, nf))
         copy.start()
         ecopies.append(copy)
-    jcopies = []
-    for d in range(1, REACH + 1):
-        copy = remote(jsend, jrecv.at[d - 1], j_s.at[d], j_r.at[d], "frag", lax.rem(me + d, nf))
-        jcopies.append(copy)
-        pl.when(me + d < nf)(copy.start)
 
     for copy in ecopies:
         copy.wait_recv()
@@ -226,10 +268,18 @@
                     total += jnp.where(hit, jrecv[d - 1, t].astype(F32) + base, 0.0)
                 acc[k] = total
 
+    if paired:
+        for p in range(fh):
+            main, diag = pack(acc[2 * p], acc[2 * p + 1])
+            rs_src[p, :, 0:NB] = main
+            rs_src[p, :, NB:LANES] = diag
+    else:
+        for k in range(fd):
+            rs_src[k, :, 0:NB] = acc[k]
     rcopies = []
     for k in range(1, ng):
         peer = lax.rem(mg + k, ng)
-        copy = remote(acc.at[pl.ds(peer * ck, ck)], rs_recv.at[k], r_s.at[k], r_r.at[k], "grp", peer)
+        copy = remote(rs_src.at[pl.ds(peer * cu, cu)], rs_recv.at[k], r_s.at[k], r_r.at[k], "grp", peer)
         copy.start()
         rcopies.append(copy)
         copy = remote(g_all.at[mg], g_all.at[mg], g_s.at[k], g_r.at[k], "grp", peer)
@@ -237,8 +287,8 @@
         rcopies.append(copy)
     for copy in rcopies:
         copy.wait_recv()
-    mine = pl.ds(mg * ck, ck)
-    total = acc[mine]
+    mine = pl.ds(mg * cu, cu)
+    total = rs_src[mine]
     for k in range(1, ng):
         total += rs_recv[k]
     fin[mine] = total
@@ -253,7 +303,15 @@
         acopies.append(copy)
     for copy in acopies:
         copy.wait_recv()
-    out[...] = fin[...]
+    if paired:
+        for p in range(fh):
+            tile = fin[p]
+            main = tile[:, 0:NB]
+            flipped = jnp.transpose(main)
+            out[2 * p] = unpack_first(main, flipped)
+            out[2 * p + 1] = unpack_second(main, flipped, tile[:, NB : NB + 1])
+    else:
+        out[...] = fin[:, :, 0:NB]
 
     for copy in tcopies + ecopies + rcopies + acopies:
         copy.wait_send()
@@ -266,6 +324,7 @@
     fd = density.shape[0]
     nd = coupling.shape[0]
     ck = fd // ng
+    cu = ck // 2 if ck % 2 == 0 else ck
     vmem = pl.BlockSpec(memory_space=pltpu.VMEM)
     smem = pl.BlockSpec(memory_space=pltpu.SMEM)
     sem = pltpu.SemaphoreType.DMA
@@ -276,19 +335,20 @@
             jax.ShapeDtypeStruct((1, LANES), F32),
             jax.ShapeDtypeStruct((1, 1), F32),
         ),
-        in_specs=[smem] + [vmem] * 6,
+        in_specs=[smem] + [vmem] * 3 + [smem] + [vmem] * 2,
         out_specs=(vmem, vmem, vmem),
         scratch_shapes=[
             pltpu.VMEM((nf, 8, LANES), F32),
             pltpu.VMEM((nf * fd, NA, 8), F32),
-            pltpu.VMEM(((REACH + 1) * fd, NB, NB), BF16),
+            pltpu.VMEM(((REACH + 1) * fd // 2, NB, LANES), BF16),
             pltpu.VMEM((nd, 2 * NB, 2 * NB), F32),
             pltpu.VMEM((nd, 2 * NB, 2 * NB), F32),
             pltpu.VMEM((nd, NB, NB), BF16),
             pltpu.VMEM((REACH, nd, NB, NB), BF16),
             pltpu.VMEM((fd, NB, NB), F32),
-            pltpu.VMEM((ng, ck, NB, NB), F32),
-            pltpu.VMEM((fd, NB, NB), F32),
+            pltpu.VMEM((ng * cu, NB, LANES), F32),
+            pltpu.VMEM((ng, cu, NB, LANES), F32),
+            pltpu.VMEM((ng * cu, NB, LANES), F32),
             pltpu.VMEM((nf, 8, LANES), F32),
             pltpu.VMEM((ng, 8, LANES), F32),
         ]
@@ -300,11 +360,11 @@
         compiler_params=pltpu.CompilerParams(collective_id=0, has_side_effects=True, vmem_limit_bytes=40 << 20),
         name="dimer_step",
     )(
-        dimer_pairs,
+        dimer_pairs.T,
         fock_blocks.reshape(fd, NB, NB),
         density.reshape(fd, NB, NB),
         coupling.reshape(nd, NB, NB),
-        jnp.repeat(atom_counts, NA).reshape(1, LANES),
+        atom_counts,
         nuclear_charge.reshape(1, LANES),
         coords,
     )

time: 62.2 us -> 46.6 us (0.75)
  Pallas kernels: 54 us -> 39.8 us
  local copies, waits for them, and re-layouts: 5.59 us -> 4.08 us
    pallas_call x1, Pallas kernels: 54 us -> 39.8 us  [per_device(): pl.pallas_call(functools.partial(kernel, nf, ng), out_shape=(jax.ShapeDty...]
    unnamed x11 -> x12, local copies, waits for them, and re-layouts: 1.96 us -> 1.22 us
    broadcast_in_dim x1 -> x0, local copies, waits for them, and re-layouts: 0.72 us -> none  [per_device(): jnp.repeat(atom_counts, NA).reshape(1, LANES)]
where the time goes in v2:
time: 46.6 us; the launch traced here: 46.4 us
  Pallas kernels  39.8 us (85%)
  local copies, waits for them, and re-layouts  4.08 us (9%)
  between operations  2.51 us (5%)
    pallas_call x1, Pallas kernels, per_device(): pl.pallas_call(functools.partial(kernel, nf, ng), out_shape=(jax.ShapeDty...  39.8 us
    unnamed x12, local copies, waits for them, and re-layouts  1.22 us
    reshape x1, local copies, waits for them, and re-layouts, per_device(): coupling.reshape(nd, NB, NB)  1.04 us

profile of v2, /device:TPU:18, one launch (start us, length us, event | category | flops | bytes accessed | tf_op | source)
XLA Modules:
  0.0 46.4 jit_solution(14161404918302244803)
XLA Ops:
  0.6 0.0 copy-start.4
  0.6 1.0 %reshape.23.coup = bf16[4,96,96]{2,1,0:T(8,128)(2,1)S(1)} reshape(bf16[4,9216]{1,0:T(4,128)(2,1)} %param.9) | data formatting | bytes 147456 | tf_op jit(solution)/shard_map/reshape | solution.py:366
  1.7 0.0 copy-done.4
  1.7 0.0 copy-start.5
  1.7 0.2 reshape.22.dens
  1.9 0.7 %copy-done.5 = bf16[8,9216]{1,0:T(8,128)(2,1)S(1)} copy-done((bf16[8,9216]{1,0:T(8,128)(2,1)S(1)}, bf16[8,9216]{1,0:T(8,128)(2,1)}, u32[]{:S(2)}) %copy-start.5) | copy-done | bytes 147480
  2.6 0.0 copy-start
  2.6 0.0 copy-start.1
  2.6 0.0 copy-start.2
  2.6 0.0 copy-start.3
  2.6 0.2 reshape.21.fock
  2.8 0.5 %copy-done = f32[3,128]{1,0:T(4,128)S(1)} copy-done((f32[3,128]{1,0:T(4,128)S(1)}, f32[3,128]{1,0:T(4,128)}, u32[]{:S(2)}) %copy-start) | copy-done | bytes 1560
  3.3 0.0 copy-done.1
  3.3 0.0 copy-done.2
  3.3 0.0 copy-done.3
  3.3 39.8 %dimer_step.1 = (f32[8,96,96]{2,1,0:T(8,128)S(1)}, f32[1,128]{1,0:T(1,128)S(1)}, f32[1,1]{1,0:T(1,128)}) custom-call(s32[2,4]{1,0:T(2,128)S(1)} %bitcast.5, bf16[8,96,96]{2,1,0:T(8,128)(2,1)S(1)} %reshape.21.fock, bf16[8,96,96]{2,1,0:T(8,128)(2,1)S(1)} %reshape.22.dens, bf16[4,96,96]{2,1,0:T(8,128)(2,1)S(1)} %reshape.23.coup, s32[8]{0:T(128)S(1)} %copy-done.2, ...), custom_call_target="tpu_custom_call" | custom-call | tf_op jit(solution)/shard_map/dimer_step/pallas_call | solution.py:331
  43.1 0.9 %reshape.25 = f32[8,9216]{1,0:T(8,128)} reshape(f32[8,96,96]{2,1,0:T(8,128)S(1)} %get-tuple-element.6) | data formatting | bytes 589824 | tf_op jit(solution)/shard_map/reshape | solution.py:371
  44.0 0.5 %slice_bitcast_fusion = f32[4]{0:T(128)} fusion(f32[1,128]{1,0:T(1,128)S(1)} %get-tuple-element.7), kind=kLoop, calls=%fused_computation | loop fusion | bytes 32 | tf_op jit(solution)/shard_map/squeeze | solution.py:371
Async XLA Ops:
  0.6 1.1 %copy-start.4 = (bf16[8,9216]{1,0:T(8,128)(2,1)S(1)}, bf16[8,9216]{1,0:T(8,128)(2,1)}, u32[]{:S(2)}) copy-start(bf16[8,9216]{1,0:T(8,128)(2,1)} %param.7) | copy-start | bytes 442372
  1.7 0.9 %copy-start.5 = (bf16[8,9216]{1,0:T(8,128)(2,1)S(1)}, bf16[8,9216]{1,0:T(8,128)(2,1)}, u32[]{:S(2)}) copy-start(bf16[8,9216]{1,0:T(8,128)(2,1)} %param.8) | copy-start | bytes 442372
  2.6 0.7 %copy-start = (f32[3,128]{1,0:T(4,128)S(1)}, f32[3,128]{1,0:T(4,128)}, u32[]{:S(2)}) copy-start(f32[3,128]{1,0:T(4,128)} %xyz.1) | copy-start | bytes 4612
  2.6 0.7 %copy-start.1 = (s32[4,2]{0,1:T(2,128)S(1)}, s32[4,2]{0,1:T(2,128)}, u32[]{:S(2)}) copy-start(s32[4,2]{0,1:T(2,128)} %param.10) | copy-start | bytes 100
  2.6 0.7 %copy-start.2 = (s32[8]{0:T(128)S(1)}, s32[8]{0:T(128)}, u32[]{:S(2)}) copy-start(s32[8]{0:T(128)} %count.1) | copy-start | bytes 100
  2.6 0.7 %copy-start.3 = (f32[128]{0:T(128)S(1)}, f32[128]{0:T(128)}, u32[]{:S(2)}) copy-start(f32[128]{0:T(128)} %param.12) | copy-start | bytes 1540

commit v3 on v2

--- a/solution.py
+++ b/solution.py
@@ -11,7 +11,8 @@
 NA = 16
 REACH = 3
 PURIF = 12
-EARLY = 6
+EARLY = 7
+HALVES = 2
 LANES = 128
 F32 = jnp.float32
 BF16 = jnp.bfloat16
@@ -111,7 +112,7 @@
         value = jnp.sum(jnp.sum(dk * fk, axis=0, keepdims=True), axis=1, keepdims=True)
         own_energy = jnp.where(part == k, value, own_energy)
     pop = jnp.sum(gathered, axis=0, keepdims=True)
-    ids = jnp.zeros((1, LANES), F32)
+    ids = jnp.full((1, LANES), -1.0, F32)
     for t in range(nd):
         ids = jnp.where(lane == t, pairs[1, t].astype(F32), ids)
         ids = jnp.where(lane == nd + t, pairs[0, t].astype(F32), ids)
@@ -138,6 +139,12 @@
         copy = remote(halo.at[pl.ds(0, fh)], halo.at[pl.ds(d * fh, fh)], h_s.at[d], h_r.at[d], "frag", lax.rem(me + nf - d, nf))
         hcopies.append(copy)
         pl.when(me >= d)(copy.start)
+
+    for t in range(nd):
+        cross = coup[t].astype(F32)
+        fds[t, 0:NB, 0:NB] = fock[jnp.clip(pairs[0, t] - me * fd, 0, fd - 1)].astype(F32)
+        fds[t, 0:NB, NB:] = cross
+        fds[t, NB:, 0:NB] = jnp.transpose(cross)
 
     for copy in tcopies:
         copy.wait_recv()
@@ -179,19 +186,14 @@
 
     big_eye = iota((2 * NB, 2 * NB), 0) == iota((2 * NB, 2 * NB), 1)
     for t in range(nd):
-        first, second = pairs[0, t], pairs[1, t]
-        fi = fock[jnp.clip(first - me * fd, 0, fd - 1)].astype(F32) + jnp.where(eye, shifts[t][0], 0.0)
-        where_j = jnp.clip(second - me * fd, 0, (REACH + 1) * fd - 1)
+        where_j = jnp.clip(pairs[1, t] - me * fd, 0, (REACH + 1) * fd - 1)
         tile = halo[where_j >> 1].astype(F32)
         main = tile[:, 0:NB]
         flipped = jnp.transpose(main)
         even = ((iota((NB, NB), 0) * 0 + where_j) & 1) == 0
         fj = jnp.where(even, unpack_first(main, flipped), unpack_second(main, flipped, tile[:, NB : NB + 1]))
-        fj = fj + jnp.where(eye, shifts[t][1], 0.0)
-        cross = coup[t].astype(F32)
-        full = jnp.concatenate(
-            [jnp.concatenate([fi, cross], axis=1), jnp.concatenate([jnp.transpose(cross), fj], axis=1)], axis=0
-        )
+        fds[t, NB:, NB:] = fj
+        full = fds[t] + jnp.where(big_eye, jnp.concatenate(shifts[t], axis=1), 0.0)
         fds[t] = full
         trace = jnp.sum(jnp.sum(jnp.where(big_eye, full, 0.0), axis=0, keepdims=True), axis=1, keepdims=True)
         shifted = full - jnp.where(big_eye, trace / (2.0 * NB), 0.0)
@@ -234,12 +236,15 @@
         pl.when(me + d < nf)(copy.start)
 
     for k in range(fd):
-        base = jnp.where(eye, 0.5, 0.0) - dens[k].astype(F32)
         here = (me * fd + k).astype(F32)
-        total = jnp.zeros((NB, NB), F32)
+        hits = jnp.sum(jnp.where(ids == here, 1.0, 0.0), axis=1, keepdims=True)
+        for d in range(1, REACH + 1):
+            other = jnp.where(lane < nd, tbl[lax.rem(me + nf - d, nf), 7:8, :], -1.0)
+            hits += jnp.sum(jnp.where(jnp.logical_and(other == here, me >= d), 1.0, 0.0), axis=1, keepdims=True)
+        total = hits * (jnp.where(eye, 0.5, 0.0) - dens[k].astype(F32))
         for t in range(nd):
-            total += jnp.where(ids[:, nd + t : nd + t + 1] == here, 0.5 * ys[t, :NB, :NB] + base, 0.0)
-            total += jnp.where(ids[:, t : t + 1] == here, 0.5 * ys[t, NB:, NB:] + base, 0.0)
+            total += jnp.where(ids[:, nd + t : nd + t + 1] == here, 0.5 * ys[t, :NB, :NB], 0.0)
+            total += jnp.where(ids[:, t : t + 1] == here, 0.5 * ys[t, NB:, NB:], 0.0)
         acc[k] = total
 
     ecopies = []
@@ -248,12 +253,6 @@
         copy.start()
         ecopies.append(copy)
 
-    for copy in ecopies:
-        copy.wait_recv()
-    group_sum = e_all[0]
-    for c in range(1, nf):
-        group_sum += e_all[c]
-    g_all[mg] = group_sum
     for d in range(1, REACH + 1):
 
         @pl.when(me >= d)
@@ -261,11 +260,10 @@
             jcopies[d - 1].wait_recv()
             sender = tbl[lax.rem(me + nf - d, nf)]
             for k in range(fd):
-                base = jnp.where(eye, 0.5, 0.0) - dens[k].astype(F32)
                 total = acc[k]
                 for t in range(nd):
                     hit = sender[7:8, t : t + 1] == (me * fd + k).astype(F32)
-                    total += jnp.where(hit, jrecv[d - 1, t].astype(F32) + base, 0.0)
+                    total += jnp.where(hit, jrecv[d - 1, t].astype(F32), 0.0)
                 acc[k] = total
 
     if paired:
@@ -276,31 +274,49 @@
     else:
         for k in range(fd):
             rs_src[k, :, 0:NB] = acc[k]
+    rows_each = NB // HALVES
+    mine = pl.ds(mg * cu, cu)
     rcopies = []
-    for k in range(1, ng):
-        peer = lax.rem(mg + k, ng)
-        copy = remote(rs_src.at[pl.ds(peer * cu, cu)], rs_recv.at[k], r_s.at[k], r_r.at[k], "grp", peer)
-        copy.start()
-        rcopies.append(copy)
-        copy = remote(g_all.at[mg], g_all.at[mg], g_s.at[k], g_r.at[k], "grp", peer)
-        copy.start()
-        rcopies.append(copy)
-    for copy in rcopies:
+    for h in range(HALVES):
+        rows = pl.ds(h * rows_each, rows_each)
+        for k in range(1, ng):
+            peer = lax.rem(mg + k, ng)
+            s = h * ng + k
+            copy = remote(rs_src.at[pl.ds(peer * cu, cu), rows], rs_recv.at[k, :, rows], r_s.at[s], r_r.at[s], "grp", peer)
+            copy.start()
+            rcopies.append(copy)
+    for copy in ecopies:
         copy.wait_recv()
-    mine = pl.ds(mg * cu, cu)
-    total = rs_src[mine]
-    for k in range(1, ng):
-        total += rs_recv[k]
-    fin[mine] = total
+    group_sum = e_all[0]
+    for c in range(1, nf):
+        group_sum += e_all[c]
+    g_all[mg] = group_sum
+    acopies = []
+    gcopies = []
+    for h in range(HALVES):
+        rows = pl.ds(h * rows_each, rows_each)
+        for k in range(1, ng):
+            rcopies[h * (ng - 1) + k - 1].wait_recv()
+        total = rs_src[mine, rows]
+        for k in range(1, ng):
+            total += rs_recv[k, :, rows]
+        fin[mine, rows] = total
+        if h == 0:
+            for k in range(1, ng):
+                copy = remote(g_all.at[mg], g_all.at[mg], g_s.at[k], g_r.at[k], "grp", lax.rem(mg + k, ng))
+                copy.start()
+                gcopies.append(copy)
+        for k in range(1, ng):
+            s = h * ng + k
+            copy = remote(fin.at[mine, rows], fin.at[mine, rows], a_s.at[s], a_r.at[s], "grp", lax.rem(mg + k, ng))
+            copy.start()
+            acopies.append(copy)
+    for copy in gcopies:
+        copy.wait_recv()
     whole = g_all[0]
     for c in range(1, ng):
         whole += g_all[c]
     tot_out[...] = jnp.sum(whole[0:1, :], axis=1, keepdims=True)
-    acopies = []
-    for k in range(1, ng):
-        copy = remote(fin.at[mine], fin.at[mine], a_s.at[k], a_r.at[k], "grp", lax.rem(mg + k, ng))
-        copy.start()
-        acopies.append(copy)
     for copy in acopies:
         copy.wait_recv()
     if paired:
@@ -313,7 +329,7 @@
     else:
         out[...] = fin[:, :, 0:NB]
 
-    for copy in tcopies + ecopies + rcopies + acopies:
+    for copy in tcopies + ecopies + rcopies + gcopies + acopies:
         copy.wait_send()
     for d in range(1, REACH + 1):
         pl.when(me >= d)(hcopies[d - 1].wait_send)
@@ -354,7 +370,7 @@
         ]
         + [sem((nf,))] * 2
         + [sem((REACH + 1,))] * 4
-        + [sem((ng,))] * 4
+        + [sem((HALVES * ng,))] * 4
         + [sem((nf,))] * 2
         + [sem((ng,))] * 2,
         compiler_params=pltpu.CompilerParams(collective_id=0, has_side_effects=True, vmem_limit_bytes=40 << 20),

time: 46.6 us -> 44.6 us (0.957)
  Pallas kernels: 39.8 us -> 37.8 us
    pallas_call x1, Pallas kernels: 39.8 us -> 37.8 us  [per_device(): pl.pallas_call(functools.partial(kernel, nf, ng), out_shape=(jax.ShapeDty...]
where the time goes in v3:
time: 44.6 us; the launch traced here: 44.4 us
  Pallas kernels  37.8 us (85%)
  local copies, waits for them, and re-layouts  4.08 us (9%)
  between operations  2.51 us (6%)
    pallas_call x1, Pallas kernels, per_device(): pl.pallas_call(functools.partial(kernel, nf, ng), out_shape=(jax.ShapeDty...  37.8 us
    unnamed x12, local copies, waits for them, and re-layouts  1.22 us
    reshape x1, local copies, waits for them, and re-layouts, per_device(): coupling.reshape(nd, NB, NB)  1.04 us
    reshape x1, local copies, waits for them, and re-layouts, per_device(): return (out.reshape(fd, NB * NB), energies[0, :nd], total[0, 0])  0.93 us

profile of v3, /device:TPU:18, one launch (start us, length us, event | category | flops | bytes accessed | tf_op | source)
XLA Modules:
  0.0 44.4 jit_solution(9663836715744248745)
XLA Ops:
  0.6 0.0 copy-start.4
  0.6 1.0 %reshape.23.coup = bf16[4,96,96]{2,1,0:T(8,128)(2,1)S(1)} reshape(bf16[4,9216]{1,0:T(4,128)(2,1)} %param.9) | data formatting | bytes 147456 | tf_op jit(solution)/shard_map/reshape | solution.py:382
  1.7 0.0 copy-done.4
  1.7 0.0 copy-start.5
  1.7 0.2 reshape.22.dens
  1.9 0.7 %copy-done.5 = bf16[8,9216]{1,0:T(8,128)(2,1)S(1)} copy-done((bf16[8,9216]{1,0:T(8,128)(2,1)S(1)}, bf16[8,9216]{1,0:T(8,128)(2,1)}, u32[]{:S(2)}) %copy-start.5) | copy-done | bytes 147480
  2.6 0.0 copy-start
  2.6 0.0 copy-start.1
  2.6 0.0 copy-start.2
  2.6 0.0 copy-start.3
  2.6 0.2 reshape.21.fock
  2.8 0.5 %copy-done = f32[3,128]{1,0:T(4,128)S(1)} copy-done((f32[3,128]{1,0:T(4,128)S(1)}, f32[3,128]{1,0:T(4,128)}, u32[]{:S(2)}) %copy-start) | copy-done | bytes 1560
  3.3 0.0 copy-done.1
  3.3 0.0 copy-done.2
  3.3 0.0 copy-done.3
  3.3 37.8 %dimer_step.1 = (f32[8,96,96]{2,1,0:T(8,128)S(1)}, f32[1,128]{1,0:T(1,128)S(1)}, f32[1,1]{1,0:T(1,128)}) custom-call(s32[2,4]{1,0:T(2,128)S(1)} %bitcast.5, bf16[8,96,96]{2,1,0:T(8,128)(2,1)S(1)} %reshape.21.fock, bf16[8,96,96]{2,1,0:T(8,128)(2,1)S(1)} %reshape.22.dens, bf16[4,96,96]{2,1,0:T(8,128)(2,1)S(1)} %reshape.23.coup, s32[8]{0:T(128)S(1)} %copy-done.2, ...), custom_call_target="tpu_custom_call" | custom-call | tf_op jit(solution)/shard_map/dimer_step/pallas_call | solution.py:347
  41.1 0.9 %reshape.25 = f32[8,9216]{1,0:T(8,128)} reshape(f32[8,96,96]{2,1,0:T(8,128)S(1)} %get-tuple-element.6) | data formatting | bytes 589824 | tf_op jit(solution)/shard_map/reshape | solution.py:387
  42.1 0.5 %slice_bitcast_fusion = f32[4]{0:T(128)} fusion(f32[1,128]{1,0:T(1,128)S(1)} %get-tuple-element.7), kind=kLoop, calls=%fused_computation | loop fusion | bytes 32 | tf_op jit(solution)/shard_map/squeeze | solution.py:387
Async XLA Ops:
  0.6 1.1 %copy-start.4 = (bf16[8,9216]{1,0:T(8,128)(2,1)S(1)}, bf16[8,9216]{1,0:T(8,128)(2,1)}, u32[]{:S(2)}) copy-start(bf16[8,9216]{1,0:T(8,128)(2,1)} %param.7) | copy-start | bytes 442372
  1.7 0.9 %copy-start.5 = (bf16[8,9216]{1,0:T(8,128)(2,1)S(1)}, bf16[8,9216]{1,0:T(8,128)(2,1)}, u32[]{:S(2)}) copy-start(bf16[8,9216]{1,0:T(8,128)(2,1)} %param.8) | copy-start | bytes 442372
  2.6 0.7 %copy-start = (f32[3,128]{1,0:T(4,128)S(1)}, f32[3,128]{1,0:T(4,128)}, u32[]{:S(2)}) copy-start(f32[3,128]{1,0:T(4,128)} %xyz.1) | copy-start | bytes 4612
  2.6 0.7 %copy-start.1 = (s32[4,2]{0,1:T(2,128)S(1)}, s32[4,2]{0,1:T(2,128)}, u32[]{:S(2)}) copy-start(s32[4,2]{0,1:T(2,128)} %param.10) | copy-start | bytes 100
  2.6 0.7 %copy-start.2 = (s32[8]{0:T(128)S(1)}, s32[8]{0:T(128)}, u32[]{:S(2)}) copy-start(s32[8]{0:T(128)} %count.1) | copy-start | bytes 100
  2.6 0.7 %copy-start.3 = (f32[128]{0:T(128)S(1)}, f32[128]{0:T(128)}, u32[]{:S(2)}) copy-start(f32[128]{0:T(128)} %param.12) | copy-start | bytes 1540

commit v4 on v3

--- a/solution.py
+++ b/solution.py
@@ -12,6 +12,7 @@
 REACH = 3
 PURIF = 12
 EARLY = 7
+LATE = 1
 HALVES = 2
 LANES = 128
 F32 = jnp.float32
@@ -35,6 +36,11 @@
     lh, ll = left
     rh, rl = right
     return dot(lh, rh) + (dot(lh, rl) + dot(ll, rh))
+
+
+def product2(left, right):
+    lh, ll = left
+    return dot(lh, right) + dot(ll, right)
 
 
 def product1(left, right):
@@ -215,7 +221,16 @@
         return carry
 
     lax.fori_loop(0, EARLY, purify_early, 0)
-    lax.fori_loop(EARLY, PURIF, purify, 0)
+    def purify_middle(index, carry):
+        for t in range(nd):
+            y = ys[t]
+            halves = split(y)
+            square = product2(halves, halves[0])
+            ys[t] = 1.5 * y - 0.5 * product2(split(square), halves[0])
+        return carry
+
+    lax.fori_loop(EARLY, PURIF - LATE, purify_middle, 0)
+    lax.fori_loop(PURIF - LATE, PURIF, purify, 0)
 
     energies = jnp.zeros((1, LANES), F32)
     for t in range(nd):
@@ -227,7 +242,7 @@
         both = jnp.sum(jnp.sum(trace + y * full, axis=0, keepdims=True), axis=1, keepdims=True)
         energies = jnp.where(lane == t, 0.5 * both - off_energy[t], energies)
     e_all[me] = jnp.broadcast_to(energies, (8, LANES))
-    eng_out[...] = energies
+    eng_out[...] = energies[:, :nd]
 
     jcopies = []
     for d in range(1, REACH + 1):
@@ -348,7 +363,7 @@
         functools.partial(kernel, nf, ng),
         out_shape=(
             jax.ShapeDtypeStruct((fd, NB, NB), F32),
-            jax.ShapeDtypeStruct((1, LANES), F32),
+            jax.ShapeDtypeStruct((1, nd), F32),
             jax.ShapeDtypeStruct((1, 1), F32),
         ),
         in_specs=[smem] + [vmem] * 3 + [smem] + [vmem] * 2,
@@ -384,7 +399,7 @@
         nuclear_charge.reshape(1, LANES),
         coords,
     )
-    return out.reshape(fd, NB * NB), energies[0, :nd], total[0, 0]
+    return out.reshape(fd, NB * NB), energies.reshape(nd), total.reshape(())
 
 
 def solution(mesh):

time: 44.6 us -> 43.4 us (0.973)
  Pallas kernels: 37.8 us -> 36.6 us
    pallas_call x1, Pallas kernels: 37.8 us -> 36.6 us  [per_device(): pl.pallas_call(functools.partial(kernel, nf, ng), out_shape=(jax.ShapeDty...]
    squeeze x1 -> x0, local copies, waits for them, and re-layouts: 0.51 us -> none  [per_device(): return (out.reshape(fd, NB * NB), energies[0, :nd], total[0, 0])]
    unnamed x12 -> x13, local copies, waits for them, and re-layouts: 1.22 us -> 1.73 us
where the time goes in v4:
time: 43.4 us; the launch traced here: 43.2 us
  Pallas kernels  36.6 us (84%)
  local copies, waits for them, and re-layouts  4.08 us (9%)
  between operations  2.51 us (6%)
    pallas_call x1, Pallas kernels, per_device(): pl.pallas_call(functools.partial(kernel, nf, ng), out_shape=(jax.ShapeDty...  36.6 us
    unnamed x13, local copies, waits for them, and re-layouts  1.73 us
    reshape x1, local copies, waits for them, and re-layouts, per_device(): coupling.reshape(nd, NB, NB)  1.04 us
    reshape x1, local copies, waits for them, and re-layouts, per_device(): return (out.reshape(fd, NB * NB), energies.reshape(nd), total.reshape(()))  0.93 us

profile of v4, /device:TPU:18, one launch (start us, length us, event | category | flops | bytes accessed | tf_op | source)
XLA Modules:
  0.0 43.2 jit_solution(10198783921007580883)
XLA Ops:
  0.6 0.0 copy-start.4
  0.6 1.0 %reshape.29.coup = bf16[4,96,96]{2,1,0:T(8,128)(2,1)S(1)} reshape(bf16[4,9216]{1,0:T(4,128)(2,1)} %param.9) | data formatting | bytes 147456 | tf_op jit(solution)/shard_map/reshape | solution.py:397
  1.7 0.0 copy-done.4
  1.7 0.0 copy-start.5
  1.7 0.2 reshape.28.dens
  1.9 0.7 %copy-done.5 = bf16[8,9216]{1,0:T(8,128)(2,1)S(1)} copy-done((bf16[8,9216]{1,0:T(8,128)(2,1)S(1)}, bf16[8,9216]{1,0:T(8,128)(2,1)}, u32[]{:S(2)}) %copy-start.5) | copy-done | bytes 147480
  2.6 0.0 copy-start
  2.6 0.0 copy-start.1
  2.6 0.0 copy-start.2
  2.6 0.0 copy-start.3
  2.6 0.2 reshape.27.fock
  2.8 0.5 %copy-done = f32[3,128]{1,0:T(4,128)S(1)} copy-done((f32[3,128]{1,0:T(4,128)S(1)}, f32[3,128]{1,0:T(4,128)}, u32[]{:S(2)}) %copy-start) | copy-done | bytes 1560
  3.3 0.0 copy-done.1
  3.3 0.0 copy-done.2
  3.3 0.0 copy-done.3
  3.3 36.6 %dimer_step.1 = (f32[8,96,96]{2,1,0:T(8,128)S(1)}, f32[1,4]{1,0:T(1,128)S(1)}, f32[1,1]{1,0:T(1,128)}) custom-call(s32[2,4]{1,0:T(2,128)S(1)} %bitcast.4, bf16[8,96,96]{2,1,0:T(8,128)(2,1)S(1)} %reshape.27.fock, bf16[8,96,96]{2,1,0:T(8,128)(2,1)S(1)} %reshape.28.dens, bf16[4,96,96]{2,1,0:T(8,128)(2,1)S(1)} %reshape.29.coup, s32[8]{0:T(128)S(1)} %copy-done.2, ...), custom_call_target="tpu_custom_call" | custom-call | tf_op jit(solution)/shard_map/dimer_step/pallas_call | solution.py:362
  40.0 0.9 %reshape.31 = f32[8,9216]{1,0:T(8,128)} reshape(f32[8,96,96]{2,1,0:T(8,128)S(1)} %get-tuple-element.6) | data formatting | bytes 589824 | tf_op jit(solution)/shard_map/reshape | solution.py:402
  40.9 0.5 %copy.12 = f32[4]{0:T(128)} copy(f32[4]{0:T(128)S(1)} %bitcast.6) | data formatting | bytes 32
Async XLA Ops:
  0.6 1.1 %copy-start.4 = (bf16[8,9216]{1,0:T(8,128)(2,1)S(1)}, bf16[8,9216]{1,0:T(8,128)(2,1)}, u32[]{:S(2)}) copy-start(bf16[8,9216]{1,0:T(8,128)(2,1)} %param.7) | copy-start | bytes 442372
  1.7 0.9 %copy-start.5 = (bf16[8,9216]{1,0:T(8,128)(2,1)S(1)}, bf16[8,9216]{1,0:T(8,128)(2,1)}, u32[]{:S(2)}) copy-start(bf16[8,9216]{1,0:T(8,128)(2,1)} %param.8) | copy-start | bytes 442372
  2.6 0.7 %copy-start = (f32[3,128]{1,0:T(4,128)S(1)}, f32[3,128]{1,0:T(4,128)}, u32[]{:S(2)}) copy-start(f32[3,128]{1,0:T(4,128)} %xyz.1) | copy-start | bytes 4612
  2.6 0.7 %copy-start.1 = (s32[4,2]{0,1:T(2,128)S(1)}, s32[4,2]{0,1:T(2,128)}, u32[]{:S(2)}) copy-start(s32[4,2]{0,1:T(2,128)} %param.10) | copy-start | bytes 100
  2.6 0.7 %copy-start.2 = (s32[8]{0:T(128)S(1)}, s32[8]{0:T(128)}, u32[]{:S(2)}) copy-start(s32[8]{0:T(128)} %count.1) | copy-start | bytes 100
  2.6 0.7 %copy-start.3 = (f32[128]{0:T(128)S(1)}, f32[128]{0:T(128)}, u32[]{:S(2)}) copy-start(f32[128]{0:T(128)} %param.12) | copy-start | bytes 1540
